TPU v7x, 32 devices: a whole 2x2x4 slice. The times are simulated.
32 devices in a mesh: gx: 4 (over y, core), gy: 8 (over z, x).
Axes of the slice: x: 2, y: 2, z: 4, core: 2. Of those that a mesh axis runs over, the one named last changes fastest.
Arguments:
- tokens: bfloat16 [256, 8192], P('gy', 'gx'), may hold values from -12 to 12
- w_gate: bfloat16 [8192, 28672], P('gx', 'gy'), may hold values from -0.0625 to 0.0625
- w_up: bfloat16 [8192, 28672], P('gx', 'gy'), may hold values from -0.0625 to 0.0625
- w_down: bfloat16 [28672, 8192], P('gy', 'gx'), may hold values from -0.03125 to 0.03125
- w_head: bfloat16 [8192, 1024], P('gx'), may hold values from -0.0625 to 0.0625
- partner: int32 [256], replicated, may hold values from 0 to 255, as said below
Outputs:
- block_out: bfloat16 [256, 8192], P('gy', 'gx')
- pair_loss: float32 [], replicated
- grad_gate: bfloat16 [8192, 28672], P('gx', 'gy')
- grad_up: bfloat16 [8192, 28672], P('gx', 'gy')
- grad_down: bfloat16 [28672, 8192], P('gy', 'gx')
- grad_head: bfloat16 [8192, 1024], P('gx', 'gy')
Inputs may be any that keep to these rules, and one draw needn't show every extreme that they name: partner[i] differs from i, and every token is the partner of exactly one token.
All inputs are finite; a program needn't handle non-finite values.
Results may differ from a plain program's by a relative error of at most 0.029.
Values may be sent and summed in bfloat16 or wider, within the bound.
A program may use at most 256 MiB of HBM per device.

v0:
```python
import math

import jax
import jax.numpy as jnp
from jax import lax
from jax.sharding import PartitionSpec as P


def contract_lead(left_mat, right_mat):
    return lax.dot_general(
        left_mat, right_mat, (((0,), (0,)), ((), ())), preferred_element_type=jnp.float32
    )


def contract_last(left_mat, right_mat):
    return lax.dot_general(
        left_mat, right_mat, (((1,), (1,)), ((), ())), preferred_element_type=jnp.float32
    )


def score_rows(proj_all, partner, row_count, score_scale):
    token_count = proj_all.shape[0]
    scores = contract_last(proj_all, proj_all) * score_scale
    row_ids = jnp.arange(row_count, dtype=jnp.int32)
    col_ids = jnp.arange(token_count, dtype=jnp.int32)
    scores = jnp.where(row_ids[:, None] == col_ids[None, :], -jnp.inf, scores)
    row_max = jnp.max(scores, axis=1, keepdims=True)
    log_total = row_max[:, 0] + jnp.log(jnp.sum(jnp.exp(scores - row_max), axis=1))
    is_partner = col_ids[None, :] == partner[:, None]
    positive = jnp.sum(jnp.where(is_partner, scores, 0.0), axis=1)
    weights_grad = (jnp.exp(scores - log_total[:, None]) - is_partner.astype(jnp.float32)).astype(
        jnp.bfloat16
    )
    return (weights_grad, log_total - positive)


def per_device(tokens, w_gate, w_up, w_down, w_head, partner):
    tok_share = tokens.shape[0]
    head_width = w_head.shape[1]
    score_scale = 1.0 / math.sqrt(head_width)
    rows_all = lax.all_gather(tokens, "gy", axis=0, tiled=True)
    token_count = rows_all.shape[0]
    row_share = token_count // lax.axis_size("gx")
    x_first = lax.axis_index("gx") * row_share
    gate_all, up_all = (
        lax.psum(
            jnp.dot(rows_all, w_gate, preferred_element_type=jnp.float32).astype(jnp.bfloat16), "gx"
        ).astype(jnp.float32),
        lax.psum(
            jnp.dot(rows_all, w_up, preferred_element_type=jnp.float32).astype(jnp.bfloat16), "gx"
        ).astype(jnp.float32),
    )
    hidden_all = (gate_all * jax.nn.sigmoid(gate_all) * up_all).astype(jnp.bfloat16)
    gate_mine = lax.dynamic_slice_in_dim(gate_all, x_first, row_share, 0)
    up_mine = lax.dynamic_slice_in_dim(up_all, x_first, row_share, 0)
    picked = hidden_all
    down_out = lax.psum_scatter(
        jnp.dot(picked, w_down, preferred_element_type=jnp.float32).astype(jnp.bfloat16),
        "gy",
        scatter_dimension=0,
        tiled=True,
    ).astype(jnp.float32)
    block_out = (tokens.astype(jnp.float32) + down_out).astype(jnp.bfloat16)
    projected = lax.psum(
        jnp.dot(block_out, w_head, preferred_element_type=jnp.float32).astype(jnp.bfloat16), "gx"
    )
    proj_all = lax.all_gather(projected, "gy", axis=0, tiled=True)
    first_row = lax.axis_index("gy") * tok_share
    weights_all, row_loss = score_rows(proj_all, partner, token_count, score_scale)
    mine_rows = lax.dynamic_slice_in_dim(weights_all, first_row, tok_share, 0)
    mine_cols = lax.dynamic_slice_in_dim(weights_all, first_row, tok_share, 1)
    row_part = jnp.dot(mine_rows, proj_all, preferred_element_type=jnp.float32)
    column_part = contract_lead(mine_cols, proj_all)
    pair_loss = jnp.sum(row_loss) / token_count
    grad_proj = ((row_part + column_part) * score_scale).astype(jnp.bfloat16)
    grad_block = contract_last(grad_proj, w_head).astype(jnp.bfloat16)
    grad_head = lax.psum_scatter(
        contract_lead(block_out, grad_proj).astype(jnp.bfloat16),
        "gy",
        scatter_dimension=1,
        tiled=True,
    )
    block_grads = lax.all_gather(grad_block, "gy", axis=0, tiled=True)
    grad_down = contract_lead(hidden_all, block_grads).astype(jnp.bfloat16)
    picked = block_grads
    grad_hidden = lax.psum_scatter(
        contract_last(picked, w_down).astype(jnp.bfloat16), "gx", scatter_dimension=0, tiled=True
    ).astype(jnp.float32)
    sigmoid_gate = jax.nn.sigmoid(gate_mine)
    grad_gate_pre = (
        grad_hidden * up_mine * sigmoid_gate * (1.0 + gate_mine * (1.0 - sigmoid_gate))
    ).astype(jnp.bfloat16)
    grad_up_pre = (grad_hidden * gate_mine * sigmoid_gate).astype(jnp.bfloat16)
    gate_grads, up_grads = (
        lax.all_gather(grad_gate_pre, "gx", axis=0, tiled=True),
        lax.all_gather(grad_up_pre, "gx", axis=0, tiled=True),
    )
    grad_gate = contract_lead(rows_all, gate_grads).astype(jnp.bfloat16)
    grad_up = contract_lead(rows_all, up_grads).astype(jnp.bfloat16)
    return (block_out, pair_loss, grad_gate, grad_up, grad_down, grad_head)


def solution(mesh):
    in_specs = (P("gy", "gx"), P("gx", "gy"), P("gx", "gy"), P("gy", "gx"), P("gx", None), P())
    out_specs = (P("gy", "gx"), P(), P("gx", "gy"), P("gx", "gy"), P("gy", "gx"), P("gx", "gy"))
    return jax.shard_map(
        per_device, mesh=mesh, in_specs=in_specs, out_specs=out_specs, check_vma=False
    )
```

profile of v0, /device:TPU:0, one launch (start us, length us, event | category | flops | bytes accessed | tf_op | source)
XLA Modules:
  0.0 527.0 jit_solution(3588408594306243018)
XLA Ops:
  7.2 0.0 all-gather.5.cloned.1.call-start
  7.2 0.7 all-gather.5.cloned.1.call-update
  7.9 0.0 all-reduce.6.cloned.1.call-start
  7.9 45.1 %all-gather.5.cloned.1.call-done = bf16[256,2048]{1,0:T(8,128)(2,1)} async-done(((bf16[32,2048]{1,0:T(8,128)(2,1)}), bf16[256,2048]{1,0:T(8,128)(2,1)}) %all-gather.5.cloned.1.call-update) | async-done | bytes 1048592 | tf_op jit(solution)/shard_map/all_gather | solution.py:41
  53.0 0.0 copy-start
  53.0 10.8 %convolution_convert_fusion.4 = bf16[256,3584]{1,0:T(8,128)(2,1)} fusion(bf16[256,2048]{1,0:T(8,128)(2,1)} %all-gather.5.cloned.1.call-done, bf16[2048,3584]{1,0:T(8,128)(2,1)} %param.8), kind=kOutput, calls=%fused_computation.6 | convolution fusion | flops 3759013888 | bytes 17563648 | tf_op jit(solution)/shard_map/dot_general | solution.py:50
  63.8 0.0 copy-done
  63.8 10.3 %convolution_convert_fusion.5 = bf16[256,3584]{1,0:T(8,128)(2,1)} fusion(bf16[256,2048]{1,0:T(8,128)(2,1)S(1)} %copy-done, bf16[2048,3584]{1,0:T(8,128)(2,1)} %param.7), kind=kOutput, calls=%fused_computation.7 | convolution fusion | flops 3759013888 | bytes 17563648 | tf_op jit(solution)/shard_map/dot_general | solution.py:47
  74.0 0.0 all-reduce.6.cloned.1.call-update
  74.1 0.0 reduce-scatter.6.cloned.1.call-start
  74.1 76.0 %all-reduce.6.cloned.1.call-done = (bf16[256,3584]{1,0:T(8,128)(2,1)}, bf16[256,3584]{1,0:T(8,128)(2,1)}) async-done(((bf16[256,3584]{1,0:T(8,128)(2,1)}, bf16[256,3584]{1,0:T(8,128)(2,1)}), (bf16[256,3584]{1,0:T(8,128)(2,1)}, bf16[256,3584]{1,0:T(8,128)(2,1)})) %all-reduce.6.cloned.1.call-update) | async-done | bytes 3670032 | tf_op jit(solution)/shard_map/psum | solution.py:49
  150.1 0.0 copy-start.3
  150.1 11.6 %convolution_convert_fusion.7 = bf16[256,2048]{1,0:T(8,128)(2,1)} fusion(bf16[3584,2048]{1,0:T(8,128)(2,1)} %param.9, bf16[256,3584]{1,0:T(8,128)(2,1)} %get-tuple-element.20, bf16[256,3584]{1,0:T(8,128)(2,1)} %get-tuple-element.21), kind=kOutput, calls=%fused_computation.10 | convolution fusion | flops 3765960704 | bytes 19398656 | tf_op jit(solution)/shard_map/dot_general | solution.py:58
  161.7 0.0 reduce-scatter.6.cloned.1.call-update
  161.7 0.0 copy-start.4
  161.8 0.0 all-reduce.4.cloned.1.call-start
  161.8 63.7 %reduce-scatter.6.cloned.1.call-done = bf16[32,2048]{1,0:T(8,128)(2,1)} async-done(((bf16[256,2048]{1,0:T(8,128)(2,1)}), bf16[32,2048]{1,0:T(8,128)(2,1)}) %reduce-scatter.6.cloned.1.call-update) | async-done | bytes 131088 | tf_op jit(solution)/shard_map/reduce_scatter | solution.py:57
  225.5 0.0 copy-done.3
  225.5 0.9 add_convert_fusion
  226.5 0.0 copy-start.2
  226.5 3.7 convolution_convert_fusion.9
  230.2 0.0 all-reduce.4.cloned.1.call-update
  230.2 0.0 all-gather.7.cloned.1.call-start
  230.2 30.1 %all-reduce.4.cloned.1.call-done = bf16[32,1024]{1,0:T(8,128)(2,1)} async-done(((bf16[32,1024]{1,0:T(8,128)(2,1)}), bf16[32,1024]{1,0:T(8,128)(2,1)}) %all-reduce.4.cloned.1.call-update) | async-done | bytes 65552 | tf_op jit(solution)/shard_map/psum | solution.py:64
  260.4 31.6 %all_gather.16 = bf16[256,1024]{1,0:T(8,128)(2,1)S(1)} all-gather(bf16[32,1024]{1,0:T(8,128)(2,1)} %all-reduce.4.cloned.1.call-done), channel_id=1, replica_groups=mesh['gx'=4,'gy'=8] {'gy'}, dimensions={0}, use_global_device_ids=true | all-gather | bytes 589824 | tf_op jit(solution)/shard_map/all_gather | solution.py:67
  292.0 0.4 fusion.15
  292.3 0.0 copy-done.4
  292.3 0.1 select_reduce_fusion
  292.4 0.6 subtract_reduce_fusion
  293.0 0.1 subtract_convert_fusion
  293.1 0.3 fusion.10
  293.4 0.2 fusion.4
  293.6 4.2 convolution_convert_fusion.8
  297.8 0.0 all-gather.7.cloned.1.call-update
  297.8 0.2 reduce-scatter.8.cloned.1.call-start
  298.0 40.0 %all-gather.7.cloned.1.call-done = bf16[256,2048]{1,0:T(8,128)(2,1)} async-done(((bf16[32,2048]{1,0:T(8,128)(2,1)}), bf16[256,2048]{1,0:T(8,128)(2,1)}) %all-gather.7.cloned.1.call-update) | async-done | bytes 1048592 | tf_op jit(solution)/shard_map/all_gather | solution.py:83
  338.0 10.7 %convolution_convert_fusion.3 = bf16[256,3584]{1,0:T(8,128)(2,1)} fusion(bf16[256,2048]{1,0:T(8,128)(2,1)} %all-gather.7.cloned.1.call-done, bf16[3584,2048]{1,0:T(8,128)(2,1)} %param.9), kind=kOutput, calls=%fused_computation.5 | convolution fusion | flops 3759013888 | bytes 17563648 | tf_op jit(solution)/shard_map/dot_general | solution.py:16
  348.8 0.0 copy-start.1
  348.8 0.0 reduce-scatter.8.cloned.1.call-update
  348.8 0.0 all-gather.9.cloned.1.call-start
  348.8 3.9 convert_element_type.74
  352.7 0.0 copy-done.1
  352.7 2.3 convert_element_type.76
  355.0 22.5 %reduce-scatter.8.cloned.1.call-done = bf16[64,3584]{1,0:T(8,128)(2,1)} async-done(((bf16[256,3584]{1,0:T(8,128)(2,1)}), bf16[64,3584]{1,0:T(8,128)(2,1)}) %reduce-scatter.8.cloned.1.call-update) | async-done | bytes 458768 | tf_op jit(solution)/shard_map/reduce_scatter | solution.py:86
  377.5 2.9 fusion.9
  380.4 0.0 all-gather.9.cloned.1.call-update
  380.4 0.0 all-gather.11.cloned.1.call-start
  380.5 0.7 all-gather.11.cloned.1.call-update
  381.2 0.0 reduce-scatter.10.cloned.1.call-start
  381.2 0.0 copy-done.2
  381.3 3.3 convolution_convert_fusion.6
  384.5 6.5 %copy.16 = bf16[2048,1024]{0,1:T(8,128)(2,1)} copy(bf16[2048,1024]{1,0:T(8,128)(2,1)} %convolution_convert_fusion.6) | data formatting | bytes 8388608
  391.1 0.0 reduce-scatter.10.cloned.1.call-update
  391.7 11.7 %convolution_convert_fusion = bf16[3584,2048]{1,0:T(8,128)(2,1)} fusion(bf16[256,2048]{1,0:T(8,128)(2,1)} %all-gather.7.cloned.1.call-done, bf16[256,3584]{1,0:T(8,128)(2,1)S(1)} %copy-done.1, bf16[256,3584]{1,0:T(8,128)(2,1)} %get-tuple-element.21), kind=kOutput, calls=%fused_computation | convolution fusion | flops 3772776448 | bytes 19398656 | tf_op jit(solution)/shard_map/dot_general | solution.py:10
  403.5 0.0 all-gather.9.cloned.1.call-done
  403.5 9.1 %fusion = bf16[2048,3584]{0,1:T(8,128)(2,1)} fusion(bf16[256,3584]{1,0:T(8,128)(2,1)} %all-gather.9.cloned.1.call-done, bf16[256,2048]{1,0:T(8,128)(2,1)S(1)} %copy-done), kind=kOutput, calls=%fused_computation.3 | convolution fusion | flops 3765436416 | bytes 17563648 | tf_op jit(solution)/shard_map/dot_general | solution.py:10
  412.5 18.7 %copy.14 = bf16[2048,3584]{1,0:T(8,128)(2,1)} copy(bf16[2048,3584]{0,1:T(8,128)(2,1)} %fusion) | data formatting | bytes 29360128
  431.2 0.0 all-gather.11.cloned.1.call-done
  431.2 8.8 %fusion.1 = bf16[2048,3584]{0,1:T(8,128)(2,1)} fusion(bf16[256,3584]{1,0:T(8,128)(2,1)} %all-gather.11.cloned.1.call-done, bf16[256,2048]{1,0:T(8,128)(2,1)S(1)} %copy-done), kind=kOutput, calls=%fused_computation.4 | convolution fusion | flops 3765436416 | bytes 17563648 | tf_op jit(solution)/shard_map/dot_general | solution.py:10
  440.0 18.8 %copy.15 = bf16[2048,3584]{1,0:T(8,128)(2,1)} copy(bf16[2048,3584]{0,1:T(8,128)(2,1)} %fusion.1) | data formatting | bytes 29360128
  458.7 58.6 %reduce-scatter.10.cloned.1.call-done = bf16[128,2048]{1,0:T(8,128)(2,1)} async-done(((bf16[1024,2048]{1,0:T(8,128)(2,1)}), bf16[128,2048]{1,0:T(8,128)(2,1)}) %reduce-scatter.10.cloned.1.call-update) | async-done | bytes 524304
  517.3 2.0 copy.17
Async XLA Ops:
  7.2 45.8 %all-gather.5.cloned.1.call-start = ((), (), s32[]{:S(2)}) async-start(), calls=%async_computation.3 | async-start | bytes 1179648 | tf_op jit(solution)/shard_map/all_gather | solution.py:41
  7.9 142.2 %all-reduce.6.cloned.1.call-start = ((), (), s32[]{:S(2)}) async-start(), calls=%async_computation.11 | async-start | bytes 7340032 | tf_op jit(solution)/shard_map/psum | solution.py:49
  53.0 10.8 %copy-start = (bf16[256,2048]{1,0:T(8,128)(2,1)S(1)}, bf16[256,2048]{1,0:T(8,128)(2,1)}, u32[]{:S(2)}) copy-start(bf16[256,2048]{1,0:T(8,128)(2,1)} %all-gather.5.cloned.1.call-done) | copy-start | bytes 3145732
  74.1 151.5 %reduce-scatter.6.cloned.1.call-start = ((), (), s32[]{:S(2)}) async-start(), calls=%async_computation.4 | async-start | bytes 1179648 | tf_op jit(solution)/shard_map/reduce_scatter | solution.py:57
  150.1 75.4 %copy-start.3 = (bf16[32,2048]{1,0:T(8,128)(2,1)S(1)}, bf16[32,2048]{1,0:T(8,128)(2,1)}, u32[]{:S(2)}) copy-start(bf16[32,2048]{1,0:T(8,128)(2,1)} %param.6) | copy-start | bytes 393220
  161.7 130.6 %copy-start.4 = (s32[256]{0:T(256)S(1)}, s32[256]{0:T(256)}, u32[]{:S(2)}) copy-start(s32[256]{0:T(256)} %param.11) | copy-start | bytes 3076
  161.8 98.6 %all-reduce.4.cloned.1.call-start = ((), (), s32[]{:S(2)}) async-start(), calls=%async_computation.5 | async-start | bytes 131072 | tf_op jit(solution)/shard_map/psum | solution.py:64
  226.5 154.8 %copy-start.2 = (bf16[32,2048]{1,0:T(8,128)(2,1)}, bf16[32,2048]{1,0:T(8,128)(2,1)S(1)}, u32[]{:S(2)}) copy-start(bf16[32,2048]{1,0:T(8,128)(2,1)S(1)} %add_convert_fusion) | copy-start | bytes 393220
  230.2 107.9 %all-gather.7.cloned.1.call-start = ((), (), s32[]{:S(2)}) async-start(), calls=%async_computation.6 | async-start | bytes 1179648 | tf_op jit(solution)/shard_map/all_gather | solution.py:83
  297.8 79.7 %reduce-scatter.8.cloned.1.call-start = ((), (), s32[]{:S(2)}) async-start(), calls=%async_computation.7 | async-start | bytes 2293760 | tf_op jit(solution)/shard_map/reduce_scatter | solution.py:86
  348.8 4.0 copy-start.1
  348.8 54.7 %all-gather.9.cloned.1.call-start = ((), (), s32[]{:S(2)}) async-start(), calls=%async_computation.8 | async-start | bytes 2293760 | tf_op jit(solution)/shard_map/all_gather | solution.py:95
  380.4 50.7 %all-gather.11.cloned.1.call-start = ((), (), s32[]{:S(2)}) async-start(), calls=%async_computation.9 | async-start | bytes 2293760 | tf_op jit(solution)/shard_map/all_gather | solution.py:96
  381.2 136.1 %reduce-scatter.10.cloned.1.call-start = ((), (), s32[]{:S(2)}) async-start(), calls=%async_computation.10 | async-start | bytes 4718592
Sparse Core Ops, SparseCore 0:
  10.1 42.8 all-gather.4
  74.2 75.9 all-reduce.5
  161.9 63.6 reduce-scatter.5
  230.3 30.0 all-reduce.3
  297.9 40.0 all-gather.6
  348.9 28.5 reduce-scatter.7
  380.6 21.1 all-gather.8
  403.9 21.1 all-gather.10
  429.2 88.0 reduce-scatter.9
where the time goes:
time: 528 us; the launch traced here: 527 us
  waiting for transfers between devices  337 us (64%)
  matrix products  84.9 us (16%)
  local copies, waits for them, and re-layouts  46 us (9%)
  blocking collectives  31.6 us (6%)
  between operations  15.7 us (3%)
  other arithmetic  10.8 us (2%)
    psum x1, waiting for transfers between devices, per_device(): lax.psum(jnp.dot(rows_all, w_up, preferred_element_type=jnp.float32).asty...  76 us
    reduce_scatter x1, waiting for transfers between devices, per_device(): lax.psum_scatter(jnp.dot(picked, w_down, preferred_element_type=jnp.float...  63.7 us
    unnamed x10, waiting for transfers between devices  60 us
    unnamed x14, local copies, waits for them, and re-layouts  46 us
    all_gather x1, waiting for transfers between devices, per_device(): rows_all = lax.all_gather(tokens, 'gy', axis=0, tiled=True)  45.1 us
    all_gather x1, waiting for transfers between devices, per_device(): block_grads = lax.all_gather(grad_block, 'gy', axis=0, tiled=True)  40 us
    dot_general x5, matrix products, contract_lead(): lax.dot_general(left_mat, right_mat, (((0,), (0,)), ((), ())), preferred_...  33.1 us
    all_gather x1, blocking collectives, per_device(): proj_all = lax.all_gather(projected, 'gy', axis=0, tiled=True)  31.6 us
  transfers between devices with their start and end apart: 9, of which 7 were waited for; matrix products, arithmetic and copies ran while one was open for 16% of the time, Pallas kernels for 0%

commit v1 on v0

v1 whole, which is shorter than its diff:
```python
import functools
import math

import jax
import jax.numpy as jnp
from jax import lax
from jax.experimental import pallas as pl
from jax.experimental.pallas import tpu as pltpu
from jax.sharding import PartitionSpec as P

F32 = jnp.float32
BF16 = jnp.bfloat16
ANY = pl.BlockSpec(memory_space=pl.ANY)
VM = pl.BlockSpec(memory_space=pltpu.VMEM)


def contract_lead(left_mat, right_mat):
    return lax.dot_general(
        left_mat, right_mat, (((0,), (0,)), ((), ())), preferred_element_type=F32
    )


def contract_last(left_mat, right_mat):
    return lax.dot_general(
        left_mat, right_mat, (((1,), (1,)), ((), ())), preferred_element_type=F32
    )


def remote(src, dst, send_sem, recv_sem, device):
    return pltpu.make_async_remote_copy(
        src_ref=src,
        dst_ref=dst,
        send_sem=send_sem,
        recv_sem=recv_sem,
        device_id=device,
        device_id_type=pl.DeviceIdType.MESH,
    )


def span(index, size):
    return pl.ds(pl.multiple_of(index * size, size), size)


def enter(gx, gy):
    ix, iy = lax.axis_index("gx"), lax.axis_index("gy")
    barrier = pltpu.get_barrier_semaphore()
    for o in range(1, gx):
        pl.semaphore_signal(
            barrier, inc=1, device_id={"gx": lax.rem(ix + o, gx)}, device_id_type=pl.DeviceIdType.MESH
        )
    for o in range(1, gy):
        pl.semaphore_signal(
            barrier, inc=1, device_id={"gy": lax.rem(iy + o, gy)}, device_id_type=pl.DeviceIdType.MESH
        )
    pl.semaphore_wait(barrier, gx + gy - 2)
    return ix, iy


class Reduce:
    def __init__(self, gx, rows, chunk, ix, refs, sems, gathered):
        self.pairs = gx // 2
        self.half, self.rows, self.chunk = rows // 2, rows // gx, chunk
        self.core = lax.rem(ix, 2)
        self.pair = lax.div(ix, 2)
        self.part, self.snd1, self.rcv1, self.own2, self.snd2, self.rcv2 = refs
        self.s1, self.r1, self.s2, self.r2, self.s3, self.r3, self.s4, self.r4 = sems
        self.out = gathered
        self.mate = {"gx": self.pair * 2 + 1 - self.core}

    def ahead(self, o):
        return lax.rem(self.pair + o, self.pairs)

    def behind(self, o):
        return lax.rem(self.pair + self.pairs - o, self.pairs)

    def peer(self, o):
        return {"gx": self.ahead(o) * 2 + self.core}

    def block(self, core, pair, c):
        at = span(core * self.pairs + pair, self.rows)
        return self.out.at[:, at, span(c, self.chunk)]

    def hop1(self, c):
        return remote(self.snd1.at[c], self.rcv1.at[c], self.s1.at[c], self.r1.at[c], self.mate)

    def hop2(self, c, o):
        return remote(
            self.snd2.at[c, o - 1], self.rcv2.at[c, o - 1],
            self.s2.at[c, o - 1], self.r2.at[c, o - 1], self.peer(o),
        )

    def hop3(self, c, o, pair):
        at = self.block(self.core, pair, c)
        return remote(at, at, self.s3.at[c, o - 1], self.r3.at[c, o - 1], self.peer(o))

    def hop4(self, c, o, core, pair):
        at = self.block(core, pair, c)
        return remote(at, at, self.s4.at[c, o], self.r4.at[c, o], self.mate)

    def send_partials(self, c):
        slot = lax.rem(c, 2)
        self.snd1[c] = self.part[slot, :, span(1 - self.core, self.half), :].astype(BF16)
        self.hop1(c).start()

    def sum_cores(self, c):
        slot = lax.rem(c, 2)
        self.hop1(c).wait_recv()
        for o in list(range(1, self.pairs)) + [0]:
            at = self.ahead(o)
            total = (
                self.part[slot, :, span(self.core * self.pairs + at, self.rows), :]
                + self.rcv1[c, :, span(at, self.rows), :].astype(F32)
            )
            if o:
                self.snd2[c, o - 1] = total.astype(BF16)
                self.hop2(c, o).start()
            else:
                self.own2[slot] = total

    def sum_pairs(self, c):
        total = self.own2[lax.rem(c, 2)]
        for o in range(1, self.pairs):
            self.hop2(c, o).wait_recv()
            total = total + self.rcv2[c, o - 1].astype(F32)
        return total

    def send_block(self, c, values):
        at = span(self.core * self.pairs + self.pair, self.rows)
        self.out[:, at, span(c, self.chunk)] = values
        for o in range(1, self.pairs):
            self.hop3(c, o, self.pair).start()
        self.hop4(c, 0, self.core, self.pair).start()

    def forward(self, c):
        for o in range(1, self.pairs):
            self.hop3(c, o, self.behind(o)).wait_recv()
            self.hop4(c, o, self.core, self.behind(o)).start()

    def arrived(self, c):
        for o in range(self.pairs):
            self.hop4(c, o, 1 - self.core, self.behind(o)).wait_recv()

    def drain(self, c):
        self.hop1(c).wait_send()
        for o in range(1, self.pairs):
            self.hop2(c, o).wait_send()
            self.hop3(c, o, self.pair).wait_send()
        for o in range(self.pairs):
            self.hop4(c, o, self.core, self.behind(o)).wait_send()

    @staticmethod
    def scratch(gx, rows, chunk, count, summed):
        pairs = gx // 2
        dma = pltpu.SemaphoreType.DMA
        far = max(pairs - 1, 1)
        return [
            pltpu.VMEM((2, summed, rows, chunk), F32),
            pltpu.VMEM((count, summed, rows // 2, chunk), BF16),
            pltpu.VMEM((count, summed, rows // 2, chunk), BF16),
            pltpu.VMEM((2, summed, rows // gx, chunk), F32),
            pltpu.VMEM((count, far, summed, rows // gx, chunk), BF16),
            pltpu.VMEM((count, far, summed, rows // gx, chunk), BF16),
        ], [
            dma((count,)), dma((count,)),
            dma((count, far)), dma((count, far)),
            dma((count, far)), dma((count, far)),
            dma((count, pairs)), dma((count, pairs)),
        ]


def when_chunk(c, count, body):
    @pl.when(jnp.logical_and(c >= 0, c < count))
    def _():
        body(c)


def forward_kernel(
    gx, gy, near, count,
    tok, w_gate, w_up, w_down, w_head,
    rows_out, gate_up_out, hidden_out, block_out, proj_out,
    rows, gate_up, hidden, block, proj, w_in, w_out, w_proj, acc, parts,
    part, snd1, rcv1, own2, snd2, rcv2,
    d_snd, d_rcv, d_snd2, d_rcv2, p_snd, p_rcv,
    s1, r1, s2, r2, s3, r3, s4, r4,
    tz_s, tz_r, tx_s, tx_r, da_s, da_r, db_s, db_r, pa_s, pa_r, pb_s, pb_r, pc_s, pc_r,
    in_sem, out_sem, head_sem, store_sem,
):
    share, width = tok.shape
    far = gy // near
    chunk = w_out.shape[1]
    head = w_head.shape[1] // 2

    def load_in(c):
        slot = lax.rem(c, 2)
        return [
            pltpu.make_async_copy(w.at[:, span(c, chunk)], w_in.at[slot, a], in_sem.at[slot, a])
            for a, w in enumerate((w_gate, w_up))
        ]

    def load_out(c):
        slot = lax.rem(c, 2)
        return pltpu.make_async_copy(w_down.at[span(c, chunk), :], w_out.at[slot], out_sem.at[slot])

    for copy in load_in(jnp.int32(0)):
        copy.start()
    load_head = pltpu.make_async_copy(w_head, w_proj, head_sem.at[0])
    load_out(jnp.int32(0)).start()
    ix, iy = enter(gx, gy)
    fz, nx = lax.div(iy, near), lax.rem(iy, near)

    def gy_at(o, p):
        return lax.rem(fz + o + far, far) * near + lax.rem(nx + p + near, near)

    def token_far(o, source):
        at = rows.at[span(source, share), :]
        return remote(at, at, tz_s.at[o - 1], tz_r.at[o - 1], {"gy": gy_at(o, 0)})

    def token_near(o, p, source):
        at = rows.at[span(source, share), :]
        return remote(at, at, tx_s.at[o, p - 1], tx_r.at[o, p - 1], {"gy": gy_at(0, p)})

    rows[span(iy, share), :] = tok[...]
    for o in range(1, far):
        token_far(o, iy).start()
    for p in range(1, near):
        token_near(0, p, iy).start()
    load_head.start()
    for o in range(1, far):
        token_far(o, gy_at(-o, 0)).wait_recv()
        for p in range(1, near):
            token_near(o, p, gy_at(-o, 0)).start()
    for o in range(far):
        for p in range(1, near):
            token_near(o, p, gy_at(-o, -p)).wait_recv()
    stores = [pltpu.make_async_copy(rows, rows_out, store_sem.at[0])]
    stores[0].start()

    acc[...] = jnp.zeros_like(acc)
    red = Reduce(
        gx, rows.shape[0], chunk, ix, (part, snd1, rcv1, own2, snd2, rcv2),
        (s1, r1, s2, r2, s3, r3, s4, r4), hidden,
    )

    def project_in(c):
        slot = lax.rem(c, 2)
        for copy in load_in(c):
            copy.wait()

        @pl.when(c + 1 < count)
        def _():
            for copy in load_in(c + 1):
                copy.start()

        for a in range(2):
            part[slot, a] = jnp.dot(rows[...], w_in[slot, a], preferred_element_type=F32)
        red.send_partials(c)

    def make_hidden(c):
        total = red.sum_pairs(c)
        gate_up[:, :, span(c, chunk)] = total
        gate, up = total[0], total[1]
        red.send_block(c, (gate * jax.nn.sigmoid(gate) * up).astype(BF16)[None])

    def project_out(c):
        slot = lax.rem(c, 2)
        red.arrived(c)
        load_out(c).wait()

        @pl.when(c + 1 < count)
        def _():
            load_out(c + 1).start()

        acc[...] += jnp.dot(
            hidden[0, :, span(c, chunk)], w_out[slot], preferred_element_type=F32
        )

    def step(s, carry):
        when_chunk(s - 1, count, red.sum_cores)
        when_chunk(s - 2, count, make_hidden)
        when_chunk(s - 3, count, red.forward)
        when_chunk(s, count, project_in)
        when_chunk(s - 4, count, project_out)
        return carry

    lax.fori_loop(0, count + 4, step, 0)
    stores.append(pltpu.make_async_copy(gate_up, gate_up_out, store_sem.at[1]))
    stores.append(pltpu.make_async_copy(hidden, hidden_out, store_sem.at[2]))
    stores[1].start()
    stores[2].start()

    def down_near(o, p):
        return remote(
            d_snd.at[o, p - 1], d_rcv.at[o, p - 1], da_s.at[o, p - 1], da_r.at[o, p - 1],
            {"gy": gy_at(0, p)},
        )

    def down_far(o):
        return remote(
            d_snd2.at[o - 1], d_rcv2.at[o - 1], db_s.at[o - 1], db_r.at[o - 1], {"gy": gy_at(o, 0)}
        )

    order = list(range(1, far)) + [0]
    for o in order:
        for p in range(1, near):
            d_snd[o, p - 1] = acc[span(gy_at(o, p), share), :].astype(BF16)
            down_near(o, p).start()
    total = None
    for o in order:
        total = acc[span(gy_at(o, 0), share), :]
        for p in range(1, near):
            down_near(o, p).wait_recv()
            total = total + d_rcv[o, p - 1].astype(F32)
        if o:
            d_snd2[o - 1] = total.astype(BF16)
            down_far(o).start()
    for o in range(1, far):
        down_far(o).wait_recv()
        total = total + d_rcv2[o - 1].astype(F32)
    block[...] = (tok[...].astype(F32) + total).astype(BF16)
    stores.append(pltpu.make_async_copy(block, block_out, store_sem.at[3]))
    stores[3].start()

    load_head.wait()
    core = red.core
    for h in range(2):
        parts[h] = jnp.dot(
            block[...], w_proj[:, h * head:(h + 1) * head], preferred_element_type=F32
        )

    def head_sum(o):
        return remote(
            p_snd.at[o - 1], p_rcv.at[o - 1], pa_s.at[o - 1], pa_r.at[o - 1],
            {"gx": lax.rem(ix + o, gx)},
        )

    def head_rows(o, source):
        at = proj.at[core, span(source, share), :]
        return remote(at, at, pb_s.at[o - 1], pb_r.at[o - 1], {"gy": lax.rem(iy + o, gy)})

    def head_mate(o, half, source):
        at = proj.at[half, span(source, share), :]
        return remote(at, at, pc_s.at[o], pc_r.at[o], red.mate)

    for o in range(1, gx):
        p_snd[o - 1] = parts[lax.rem(ix + o, 2)].astype(BF16)
        head_sum(o).start()
    total = parts[core]
    for o in range(1, gx):
        head_sum(o).wait_recv()
        total = total + p_rcv[o - 1].astype(F32)
    proj[core, span(iy, share), :] = total.astype(BF16)
    for o in range(1, gy):
        head_rows(o, iy).start()
    head_mate(0, core, iy).start()
    for o in range(1, gy):
        source = lax.rem(iy + gy - o, gy)
        head_rows(o, source).wait_recv()
        head_mate(o, core, source).start()
    for o in range(gy):
        head_mate(o, 1 - core, lax.rem(iy + gy - o, gy)).wait_recv()
    for h in range(2):
        stores.append(
            pltpu.make_async_copy(
                proj.at[h], proj_out.at[:, h * head:(h + 1) * head], store_sem.at[4 + h]
            )
        )
        stores[4 + h].start()

    def finish(c, carry):
        red.drain(c)
        return carry

    lax.fori_loop(0, count, finish, 0)
    for o in range(1, far):
        token_far(o, iy).wait_send()
        down_far(o).wait_send()
    for o in range(far):
        for p in range(1, near):
            token_near(o, p, gy_at(-o, 0)).wait_send()
            down_near(o, p).wait_send()
    for o in range(1, gx):
        head_sum(o).wait_send()
    for o in range(1, gy):
        head_rows(o, iy).wait_send()
    for o in range(gy):
        head_mate(o, core, lax.rem(iy + gy - o, gy)).wait_send()
    for copy in stores:
        copy.wait()


def backward_kernel(
    gx, gy, count,
    grad_block, block, w_down, gate_up,
    grads_out, blocks_out,
    grads, blocks, w_in,
    part, snd1, rcv1, own2, snd2, rcv2,
    s1, r1, s2, r2, s3, r3, s4, r4,
    b_s, b_r, in_sem, store_sem,
):
    share = block.shape[0]
    chunk = w_in.shape[1]

    def load_in(c):
        slot = lax.rem(c, 2)
        return pltpu.make_async_copy(w_down.at[span(c, chunk), :], w_in.at[slot], in_sem.at[slot])

    load_in(jnp.int32(0)).start()
    ix, iy = enter(gx, gy)
    red = Reduce(
        gx, grad_block.shape[0], chunk, ix, (part, snd1, rcv1, own2, snd2, rcv2),
        (s1, r1, s2, r2, s3, r3, s4, r4), grads,
    )

    def share_block(o, source):
        at = blocks.at[span(source, share), :]
        return remote(at, at, b_s.at[o - 1], b_r.at[o - 1], {"gy": lax.rem(iy + o, gy)})

    blocks[span(iy, share), :] = block[...]
    for o in range(1, gy):
        share_block(o, iy).start()

    def project(c):
        slot = lax.rem(c, 2)
        load_in(c).wait()

        @pl.when(c + 1 < count)
        def _():
            load_in(c + 1).start()

        part[slot, 0] = contract_last(grad_block[...], w_in[slot])
        red.send_partials(c)

    def make_grads(c):
        grad_hidden = red.sum_pairs(c)[0]
        gate = gate_up[0, :, span(c, chunk)]
        up = gate_up[1, :, span(c, chunk)]
        sig = jax.nn.sigmoid(gate)
        grad_gate = grad_hidden * up * sig * (1.0 + gate * (1.0 - sig))
        grad_up = grad_hidden * gate * sig
        red.send_block(c, jnp.stack([grad_gate.astype(BF16), grad_up.astype(BF16)]))

    def step(s, carry):
        when_chunk(s - 1, count, red.sum_cores)
        when_chunk(s - 2, count, make_grads)
        when_chunk(s - 3, count, red.forward)
        when_chunk(s, count, project)
        return carry

    lax.fori_loop(0, count + 3, step, 0)

    def finish(c, carry):
        red.arrived(c)
        red.drain(c)
        return carry

    lax.fori_loop(0, count, finish, 0)
    first = pltpu.make_async_copy(grads, grads_out, store_sem.at[0])
    first.start()
    for o in range(1, gy):
        share_block(o, lax.rem(iy + gy - o, gy)).wait_recv()
    second = pltpu.make_async_copy(blocks, blocks_out, store_sem.at[1])
    second.start()
    for o in range(1, gy):
        share_block(o, iy).wait_send()
    first.wait()
    second.wait()


def outer_kernel(left, right, out):
    out[...] = contract_lead(left[...], right[...]).astype(BF16)


def outer(left, right, tile):
    rows, height = left.shape
    width = right.shape[1]
    return pl.pallas_call(
        outer_kernel,
        grid=(height // tile,),
        in_specs=[
            pl.BlockSpec((rows, tile), lambda i: (0, i)),
            pl.BlockSpec((rows, width), lambda i: (0, 0)),
        ],
        out_specs=pl.BlockSpec((tile, width), lambda i: (i, 0)),
        out_shape=jax.ShapeDtypeStruct((height, width), BF16),
        compiler_params=pltpu.CompilerParams(vmem_limit_bytes=40 << 20),
        cost_estimate=pl.CostEstimate(
            flops=2 * rows * height * width,
            bytes_accessed=2 * (rows * height + rows * width + height * width),
            transcendentals=0,
        ),
    )(left, right)


def per_device(gx, gy, tokens, w_gate, w_up, w_down, w_head, partner):
    share, width = tokens.shape
    total_rows = share * gy
    hidden_width = w_gate.shape[1]
    head_width = w_head.shape[1]
    near = 1 << (int(math.log2(gy)) // 2)
    far = gy // near
    count = next(c for c in (7, 8, 4, 2, 1) if hidden_width % (128 * c) == 0)
    chunk = hidden_width // count
    own = total_rows // gx
    dma = pltpu.SemaphoreType.DMA
    shape = jax.ShapeDtypeStruct

    buffers, sems = Reduce.scratch(gx, total_rows, chunk, count, 2)
    fm, nm = max(far - 1, 1), max(near - 1, 1)
    rows_all, gate_up, hidden, block_out, proj_all = pl.pallas_call(
        functools.partial(forward_kernel, gx, gy, near, count),
        in_specs=[VM, ANY, ANY, ANY, ANY],
        out_specs=[ANY] * 5,
        out_shape=[
            shape((total_rows, width), BF16),
            shape((2, own, hidden_width), F32),
            shape((1, total_rows, hidden_width), BF16),
            shape((share, width), BF16),
            shape((total_rows, head_width), BF16),
        ],
        scratch_shapes=[
            pltpu.VMEM((total_rows, width), BF16),
            pltpu.VMEM((2, own, hidden_width), F32),
            pltpu.VMEM((1, total_rows, hidden_width), BF16),
            pltpu.VMEM((share, width), BF16),
            pltpu.VMEM((2, total_rows, head_width // 2), BF16),
            pltpu.VMEM((2, 2, width, chunk), BF16),
            pltpu.VMEM((2, chunk, width), BF16),
            pltpu.VMEM((width, head_width), BF16),
            pltpu.VMEM((total_rows, width), F32),
            pltpu.VMEM((2, share, head_width // 2), F32),
            *buffers,
            pltpu.VMEM((far, nm, share, width), BF16),
            pltpu.VMEM((far, nm, share, width), BF16),
            pltpu.VMEM((fm, share, width), BF16),
            pltpu.VMEM((fm, share, width), BF16),
            pltpu.VMEM((gx - 1, share, head_width // 2), BF16),
            pltpu.VMEM((gx - 1, share, head_width // 2), BF16),
            *sems,
            dma((fm,)), dma((fm,)), dma((far, nm)), dma((far, nm)),
            dma((far, nm)), dma((far, nm)), dma((fm,)), dma((fm,)),
            dma((gx - 1,)), dma((gx - 1,)), dma((gy - 1,)), dma((gy - 1,)),
            dma((gy,)), dma((gy,)),
            dma((2, 2)), dma((2,)), dma((1,)), dma((6,)),
        ],
        compiler_params=pltpu.CompilerParams(
            collective_id=0, has_side_effects=True, vmem_limit_bytes=56 << 20
        ),
    )(tokens, w_gate, w_up, w_down, w_head)
    hidden = hidden[0]

    scale = 1.0 / math.sqrt(head_width)
    ids = jnp.arange(total_rows, dtype=jnp.int32)
    scores = contract_last(proj_all, proj_all) * scale
    scores = jnp.where(ids[:, None] == ids[None, :], -jnp.inf, scores)
    row_max = jnp.max(scores, axis=1, keepdims=True)
    log_total = row_max[:, 0] + jnp.log(jnp.sum(jnp.exp(scores - row_max), axis=1))
    is_partner = ids[None, :] == partner[:, None]
    positive = jnp.sum(jnp.where(is_partner, scores, 0.0), axis=1)
    weights = (jnp.exp(scores - log_total[:, None]) - is_partner.astype(F32)).astype(BF16)
    pair_loss = jnp.sum(log_total - positive) / total_rows
    grad_proj = (
        (jnp.dot(weights, proj_all, preferred_element_type=F32) + contract_lead(weights, proj_all))
        * scale
    ).astype(BF16)
    grad_block = contract_last(grad_proj, w_head).astype(BF16)

    buffers, sems = Reduce.scratch(gx, total_rows, chunk, count, 1)
    grads, blocks = pl.pallas_call(
        functools.partial(backward_kernel, gx, gy, count),
        in_specs=[VM, VM, ANY, VM],
        out_specs=[ANY] * 2,
        out_shape=[
            shape((2, total_rows, hidden_width), BF16),
            shape((total_rows, width), BF16),
        ],
        scratch_shapes=[
            pltpu.VMEM((2, total_rows, hidden_width), BF16),
            pltpu.VMEM((total_rows, width), BF16),
            pltpu.VMEM((2, chunk, width), BF16),
            *buffers,
            *sems,
            dma((gy - 1,)), dma((gy - 1,)), dma((2,)), dma((2,)),
        ],
        compiler_params=pltpu.CompilerParams(
            collective_id=1, has_side_effects=True, vmem_limit_bytes=48 << 20
        ),
    )(grad_block, block_out, w_down, gate_up)

    grad_down = outer(hidden, grad_block, 256)
    grad_gate = outer(rows_all, grads[0], 256)
    grad_up = outer(rows_all, grads[1], 256)
    mine = head_width // gy
    proj_mine = lax.dynamic_slice_in_dim(grad_proj, lax.axis_index("gy") * mine, mine, 1)
    grad_head = contract_lead(blocks, proj_mine).astype(BF16)
    return (block_out, pair_loss, grad_gate, grad_up, grad_down, grad_head)


def solution(mesh):
    in_specs = (P("gy", "gx"), P("gx", "gy"), P("gx", "gy"), P("gy", "gx"), P("gx", None), P())
    out_specs = (P("gy", "gx"), P(), P("gx", "gy"), P("gx", "gy"), P("gy", "gx"), P("gx", "gy"))
    body = functools.partial(per_device, mesh.shape["gx"], mesh.shape["gy"])
    return jax.shard_map(body, mesh=mesh, in_specs=in_specs, out_specs=out_specs, check_vma=False)
```

time: 528 us -> 178 us (0.34)
  waiting for transfers between devices: 337 us -> 0 us
  Pallas kernels: 0 us -> 164 us
  matrix products: 84.9 us -> 7.17 us
  local copies, waits for them, and re-layouts: 46 us -> 2.97 us
  blocking collectives: 31.6 us -> 0 us
  between operations: 15.7 us -> 2.55 us
  other arithmetic: 10.8 us -> 0.7 us
    pallas_call x0 -> x5, Pallas kernels: none -> 164 us  [the longest x1 92.1 us: per_device(): pl.pallas_call(functools.partial(forward_kernel, gx, gy, near, count), in...]
    psum x2 -> x0, waiting for transfers between devices: 106 us -> none  [the longest x1 76 us: per_device(): lax.psum(jnp.dot(rows_all, w_up, preferred_element_type=jnp.float32).asty...]
    reduce_scatter x2 -> x0, waiting for transfers between devices: 86.2 us -> none  [the longest x1 63.7 us: per_device(): lax.psum_scatter(jnp.dot(picked, w_down, preferred_element_type=jnp.float...]
    all_gather x4 -> x0, waiting for transfers between devices: 85.1 us -> none  [the longest x1 45.1 us: per_device(): rows_all = lax.all_gather(tokens, 'gy', axis=0, tiled=True)]
    unnamed x10 -> x0, waiting for transfers between devices: 60 us -> none
    unnamed x14 -> x13, local copies, waits for them, and re-layouts: 46 us -> 0.68 us
    dot_general x5 -> x1, matrix products: 36.6 us -> 1.54 us  [per_device(): jnp.dot(weights, proj_all, preferred_element_type=F32)]
    all_gather x1 -> x0, blocking collectives: 31.6 us -> none  [per_device(): proj_all = lax.all_gather(projected, 'gy', axis=0, tiled=True)]
  transfers between devices with their start and end apart: 9 -> 0, of which waited for: 7 -> 0; matrix products, arithmetic and copies ran while one was open for 16% -> 0% of each run, Pallas kernels for 0% -> 0%
where the time goes in v1:
time: 178 us; the launch traced here: 177 us
  Pallas kernels  164 us (92%)
  matrix products  7.17 us (4%)
  local copies, waits for them, and re-layouts  2.97 us (2%)
  between operations  2.55 us (1%)
    pallas_call x1, Pallas kernels, per_device(): pl.pallas_call(functools.partial(forward_kernel, gx, gy, near, count), in...  92.1 us
    pallas_call x1, Pallas kernels, per_device(): pl.pallas_call(functools.partial(backward_kernel, gx, gy, count), in_spec...  44.5 us
    pallas_call x3, Pallas kernels, outer(): pl.pallas_call(outer_kernel, grid=(height // tile,), in_specs=[pl.BlockSp...  27.3 us

profile of v1, /device:TPU:0, one launch (start us, length us, event | category | flops | bytes accessed | tf_op | source)
XLA Modules:
  0.0 177.3 jit_solution(151887846577826820)
XLA Ops:
  0.6 0.0 copy-start.5
  0.6 92.1 %shard_map.109 = (bf16[256,2048]{1,0:T(8,128)(2,1)}, f32[2,64,3584]{2,1,0:T(8,128)}, bf16[1,256,3584]{2,1,0:T(8,128)(2,1)}, bf16[32,2048]{1,0:T(8,128)(2,1)}, bf16[256,1024]{1,0:T(8,128)(2,1)}) custom-call(bf16[32,2048]{1,0:T(8,128)(2,1)} %tok.1, bf16[2048,3584]{1,0:T(8,128)(2,1)} %w_gate.1, bf16[2048,3584]{1,0:T(8,128)(2,1)} %w_up.1, ...), custom_call_target="tpu_custom_call" | custom-call | tf_op jit(solution)/shard_map/pallas_call | solution.py:509
  92.8 1.6 fusion.6
  94.3 0.0 copy-done.5
  94.3 0.1 select_reduce_fusion
  94.4 0.6 subtract_reduce_fusion
  95.7 0.0 copy-start.4
  95.7 1.5 fusion.4
  97.2 0.0 copy-start.2
  97.3 0.0 copy-start.3
  97.3 1.5 fusion.1
  98.8 0.0 copy-done.4
  98.8 1.3 convolution_convert_fusion.grad_block.right
  100.1 0.0 copy-done.2
  100.1 0.0 copy-done.3
  100.1 44.5 %shard_map.110 = (bf16[2,256,3584]{2,1,0:T(8,128)(2,1)}, bf16[256,2048]{1,0:T(8,128)(2,1)S(1)}) custom-call(bf16[256,2048]{1,0:T(8,128)(2,1)S(1)} %convolution_convert_fusion.grad_block.right, bf16[32,2048]{1,0:T(8,128)(2,1)S(1)} %copy-done.3, bf16[3584,2048]{1,0:T(8,128)(2,1)} %w_down.3, f32[2,64,3584]{2,1,0:T(8,128)S(1)} %copy-done.2), custom_call_target="tpu_custom_call" | custom-call | tf_op jit(solution)/shard_map/pallas_call | solution.py:568
  144.6 0.0 copy-start.1
  144.6 1.3 convolution_convert_fusion.1
  145.9 2.3 %slice_bitcast_fusion = (bf16[256,3584]{1,0:T(8,128)(2,1)S(1)}, bf16[256,3584]{1,0:T(8,128)(2,1)S(1)}) fusion(bf16[2,256,3584]{2,1,0:T(8,128)(2,1)} %get-tuple-element.17), kind=kLoop, calls=%fused_computation.2 | loop fusion | bytes 7340032 | tf_op jit(solution)/shard_map/squeeze | solution.py:591
  148.2 0.0 copy-done.1
  148.2 0.0 copy-start
  148.2 10.6 %shard_map.113 = bf16[3584,2048]{1,0:T(8,128)(2,1)} custom-call(bf16[256,3584]{1,0:T(8,128)(2,1)S(1)} %bitcast.12, bf16[256,2048]{1,0:T(8,128)(2,1)S(1)} %convolution_convert_fusion.grad_block.right), custom_call_target="tpu_custom_call" | custom-call | flops 3758096384 | bytes 17563648 | tf_op jit(solution)/shard_map/pallas_call | solution.py:476
  158.8 0.0 copy-done
  158.8 8.4 %shard_map.112 = bf16[2048,3584]{1,0:T(8,128)(2,1)} custom-call(bf16[256,2048]{1,0:T(8,128)(2,1)S(1)} %copy-done, bf16[256,3584]{1,0:T(8,128)(2,1)S(1)} %get-tuple-element.24.right), custom_call_target="tpu_custom_call" | custom-call | flops 3758096384 | bytes 17563648 | tf_op jit(solution)/shard_map/pallas_call | solution.py:476
  167.1 8.4 %shard_map.111 = bf16[2048,3584]{1,0:T(8,128)(2,1)} custom-call(bf16[256,2048]{1,0:T(8,128)(2,1)S(1)} %copy-done, bf16[256,3584]{1,0:T(8,128)(2,1)S(1)} %get-tuple-element.25.right), custom_call_target="tpu_custom_call" | custom-call | flops 3758096384 | bytes 17563648 | tf_op jit(solution)/shard_map/pallas_call | solution.py:476
  175.5 0.7 copy.13
Async XLA Ops:
  0.6 93.7 %copy-start.5 = (s32[256]{0:T(256)S(1)}, s32[256]{0:T(256)}, u32[]{:S(2)}) copy-start(s32[256]{0:T(256)} %param.11) | copy-start | bytes 3076
  95.7 3.1 %copy-start.4 = (bf16[2048,1024]{1,0:T(8,128)(2,1)S(1)}, bf16[2048,1024]{1,0:T(8,128)(2,1)}, u32[]{:S(2)}) copy-start(bf16[2048,1024]{1,0:T(8,128)(2,1)} %w_head.1) | copy-start | bytes 12582916
  97.2 2.8 %copy-start.2 = (f32[2,64,3584]{2,1,0:T(8,128)S(1)}, f32[2,64,3584]{2,1,0:T(8,128)}, u32[]{:S(2)}) copy-start(f32[2,64,3584]{2,1,0:T(8,128)} %get-tuple-element.16.gate_up) | copy-start | bytes 5505028
  97.3 2.8 %copy-start.3 = (bf16[32,2048]{1,0:T(8,128)(2,1)S(1)}, bf16[32,2048]{1,0:T(8,128)(2,1)}, u32[]{:S(2)}) copy-start(bf16[32,2048]{1,0:T(8,128)(2,1)} %get-tuple-element.34.block) | copy-start | bytes 393220
  144.6 3.6 %copy-start.1 = (bf16[1,256,3584]{2,1,0:T(8,128)(2,1)S(1)}, bf16[1,256,3584]{2,1,0:T(8,128)(2,1)}, u32[]{:S(2)}) copy-start(bf16[1,256,3584]{2,1,0:T(8,128)(2,1)} %get-tuple-element.18) | copy-start | bytes 5505028
  148.2 10.6 %copy-start = (bf16[256,2048]{1,0:T(8,128)(2,1)S(1)}, bf16[256,2048]{1,0:T(8,128)(2,1)}, u32[]{:S(2)}) copy-start(bf16[256,2048]{1,0:T(8,128)(2,1)} %get-tuple-element.15.left) | copy-start | bytes 3145732

commit v2 on v1

--- a/solution.py
+++ b/solution.py
@@ -177,17 +177,18 @@
 def forward_kernel(
     gx, gy, near, count,
     tok, w_gate, w_up, w_down, w_head,
-    rows_out, gate_up_out, hidden_out, block_out, proj_out,
-    rows, gate_up, hidden, block, proj, w_in, w_out, w_proj, acc, parts,
+    rows_out, hidden_out, gate_out, up_out, block_out, proj_out,
+    rows, factors, hidden, block, proj, w_in, w_out, w_proj, acc, parts,
     part, snd1, rcv1, own2, snd2, rcv2,
     d_snd, d_rcv, d_snd2, d_rcv2, p_snd, p_rcv,
     s1, r1, s2, r2, s3, r3, s4, r4,
-    tz_s, tz_r, tx_s, tx_r, da_s, da_r, db_s, db_r, pa_s, pa_r, pb_s, pb_r, pc_s, pc_r,
+    tz_s, tz_r, tx_s, tx_r, da_s, da_r, db_s, db_r, pa_s, pa_r, pb_s, pb_r, pc_s, pc_r, fa_s, fa_r, fb_s, fb_r,
     in_sem, out_sem, head_sem, store_sem,
 ):
     share, width = tok.shape
     far = gy // near
-    chunk = w_out.shape[1]
+    chunk, deep = w_in.shape[3], w_out.shape[1]
+    group = deep // chunk
     head = w_head.shape[1] // 2
 
     def load_in(c):
@@ -197,9 +198,9 @@
             for a, w in enumerate((w_gate, w_up))
         ]
 
-    def load_out(c):
-        slot = lax.rem(c, 2)
-        return pltpu.make_async_copy(w_down.at[span(c, chunk), :], w_out.at[slot], out_sem.at[slot])
+    def load_out(g):
+        slot = lax.rem(g, 2)
+        return pltpu.make_async_copy(w_down.at[span(g, deep), :], w_out.at[slot], out_sem.at[slot])
 
     for copy in load_in(jnp.int32(0)):
         copy.start()
@@ -257,22 +258,30 @@
 
     def make_hidden(c):
         total = red.sum_pairs(c)
-        gate_up[:, :, span(c, chunk)] = total
         gate, up = total[0], total[1]
-        red.send_block(c, (gate * jax.nn.sigmoid(gate) * up).astype(BF16)[None])
+        sig = jax.nn.sigmoid(gate)
+        silu = gate * sig
+        red.send_block(c, (silu * up).astype(BF16)[None])
+        at = span(red.core * red.pairs + red.pair, red.rows)
+        factors[0, at, span(c, chunk)] = (up * sig * (1.0 + gate * (1.0 - sig))).astype(BF16)
+        factors[1, at, span(c, chunk)] = silu.astype(BF16)
 
     def project_out(c):
-        slot = lax.rem(c, 2)
         red.arrived(c)
-        load_out(c).wait()
-
-        @pl.when(c + 1 < count)
+
+        @pl.when(lax.rem(c, group) == group - 1)
         def _():
-            load_out(c + 1).start()
-
-        acc[...] += jnp.dot(
-            hidden[0, :, span(c, chunk)], w_out[slot], preferred_element_type=F32
-        )
+            g = lax.div(c, group)
+            slot = lax.rem(g, 2)
+            load_out(g).wait()
+
+            @pl.when(g + 1 < count // group)
+            def _():
+                load_out(g + 1).start()
+
+            acc[...] += jnp.dot(
+                hidden[0, :, span(g, deep)], w_out[slot], preferred_element_type=F32
+            )
 
     def step(s, carry):
         when_chunk(s - 1, count, red.sum_cores)
@@ -283,10 +292,8 @@
         return carry
 
     lax.fori_loop(0, count + 4, step, 0)
-    stores.append(pltpu.make_async_copy(gate_up, gate_up_out, store_sem.at[1]))
-    stores.append(pltpu.make_async_copy(hidden, hidden_out, store_sem.at[2]))
+    stores.append(pltpu.make_async_copy(hidden.at[0], hidden_out, store_sem.at[1]))
     stores[1].start()
-    stores[2].start()
 
     def down_near(o, p):
         return remote(
@@ -304,6 +311,18 @@
         for p in range(1, near):
             d_snd[o, p - 1] = acc[span(gy_at(o, p), share), :].astype(BF16)
             down_near(o, p).start()
+
+    def factor_pair(o, pair):
+        at = factors.at[:, span(red.core * red.pairs + pair, red.rows), :]
+        return remote(at, at, fa_s.at[o - 1], fa_r.at[o - 1], red.peer(o))
+
+    def factor_mate(o, core, pair):
+        at = factors.at[:, span(core * red.pairs + pair, red.rows), :]
+        return remote(at, at, fb_s.at[o], fb_r.at[o], red.mate)
+
+    for o in range(1, red.pairs):
+        factor_pair(o, red.pair).start()
+    factor_mate(0, red.core, red.pair).start()
     total = None
     for o in order:
         total = acc[span(gy_at(o, 0), share), :]
@@ -317,8 +336,8 @@
         down_far(o).wait_recv()
         total = total + d_rcv2[o - 1].astype(F32)
     block[...] = (tok[...].astype(F32) + total).astype(BF16)
-    stores.append(pltpu.make_async_copy(block, block_out, store_sem.at[3]))
-    stores[3].start()
+    stores.append(pltpu.make_async_copy(block, block_out, store_sem.at[2]))
+    stores[2].start()
 
     load_head.wait()
     core = red.core
@@ -361,10 +380,18 @@
     for h in range(2):
         stores.append(
             pltpu.make_async_copy(
-                proj.at[h], proj_out.at[:, h * head:(h + 1) * head], store_sem.at[4 + h]
+                proj.at[h], proj_out.at[:, h * head:(h + 1) * head], store_sem.at[3 + h]
             )
         )
-        stores[4 + h].start()
+        stores[3 + h].start()
+    for o in range(1, red.pairs):
+        factor_pair(o, red.behind(o)).wait_recv()
+        factor_mate(o, core, red.behind(o)).start()
+    for o in range(red.pairs):
+        factor_mate(o, 1 - core, red.behind(o)).wait_recv()
+    for a, out in enumerate((gate_out, up_out)):
+        stores.append(pltpu.make_async_copy(factors.at[a], out, store_sem.at[5 + a]))
+        stores[5 + a].start()
 
     def finish(c, carry):
         red.drain(c)
@@ -378,6 +405,10 @@
         for p in range(1, near):
             token_near(o, p, gy_at(-o, 0)).wait_send()
             down_near(o, p).wait_send()
+    for o in range(1, red.pairs):
+        factor_pair(o, red.pair).wait_send()
+    for o in range(red.pairs):
+        factor_mate(o, core, red.behind(o)).wait_send()
     for o in range(1, gx):
         head_sum(o).wait_send()
     for o in range(1, gy):
@@ -390,12 +421,12 @@
 
 def backward_kernel(
     gx, gy, count,
-    grad_block, block, w_down, gate_up,
-    grads_out, blocks_out,
-    grads, blocks, w_in,
+    grad_block, block, w_down, gate_in, up_in,
+    gate_out, up_out, blocks_out,
+    grads, blocks, w_in, factors, results,
     part, snd1, rcv1, own2, snd2, rcv2,
     s1, r1, s2, r2, s3, r3, s4, r4,
-    b_s, b_r, in_sem, store_sem,
+    b_s, b_r, in_sem, fac_sem, store_sem,
 ):
     share = block.shape[0]
     chunk = w_in.shape[1]
@@ -405,6 +436,12 @@
         return pltpu.make_async_copy(w_down.at[span(c, chunk), :], w_in.at[slot], in_sem.at[slot])
 
     load_in(jnp.int32(0)).start()
+    fetch = [
+        pltpu.make_async_copy(source, factors.at[a], fac_sem.at[a])
+        for a, source in enumerate((gate_in, up_in))
+    ]
+    for copy in fetch:
+        copy.start()
     ix, iy = enter(gx, gy)
     red = Reduce(
         gx, grad_block.shape[0], chunk, ix, (part, snd1, rcv1, own2, snd2, rcv2),
@@ -430,40 +467,48 @@
         part[slot, 0] = contract_last(grad_block[...], w_in[slot])
         red.send_partials(c)
 
+    def gather(c):
+        red.send_block(c, red.sum_pairs(c).astype(BF16))
+
     def make_grads(c):
-        grad_hidden = red.sum_pairs(c)[0]
-        gate = gate_up[0, :, span(c, chunk)]
-        up = gate_up[1, :, span(c, chunk)]
-        sig = jax.nn.sigmoid(gate)
-        grad_gate = grad_hidden * up * sig * (1.0 + gate * (1.0 - sig))
-        grad_up = grad_hidden * gate * sig
-        red.send_block(c, jnp.stack([grad_gate.astype(BF16), grad_up.astype(BF16)]))
+        red.arrived(c)
+        grad_hidden = grads[0, :, span(c, chunk)].astype(F32)
+        for a in range(2):
+            results[a, :, span(c, chunk)] = (
+                grad_hidden * factors[a, :, span(c, chunk)].astype(F32)
+            ).astype(BF16)
 
     def step(s, carry):
         when_chunk(s - 1, count, red.sum_cores)
-        when_chunk(s - 2, count, make_grads)
+        when_chunk(s - 2, count, gather)
         when_chunk(s - 3, count, red.forward)
         when_chunk(s, count, project)
+        when_chunk(s - 4, count, make_grads)
         return carry
 
-    lax.fori_loop(0, count + 3, step, 0)
+    for copy in fetch:
+        copy.wait()
+    lax.fori_loop(0, count + 4, step, 0)
+    stores = [
+        pltpu.make_async_copy(results.at[a], out, store_sem.at[a])
+        for a, out in enumerate((gate_out, up_out))
+    ]
+    for copy in stores:
+        copy.start()
 
     def finish(c, carry):
-        red.arrived(c)
         red.drain(c)
         return carry
 
     lax.fori_loop(0, count, finish, 0)
-    first = pltpu.make_async_copy(grads, grads_out, store_sem.at[0])
-    first.start()
     for o in range(1, gy):
         share_block(o, lax.rem(iy + gy - o, gy)).wait_recv()
-    second = pltpu.make_async_copy(blocks, blocks_out, store_sem.at[1])
-    second.start()
+    stores.append(pltpu.make_async_copy(blocks, blocks_out, store_sem.at[2]))
+    stores[2].start()
     for o in range(1, gy):
         share_block(o, iy).wait_send()
-    first.wait()
-    second.wait()
+    for copy in stores:
+        copy.wait()
 
 
 def outer_kernel(left, right, out):
@@ -498,33 +543,34 @@
     head_width = w_head.shape[1]
     near = 1 << (int(math.log2(gy)) // 2)
     far = gy // near
-    count = next(c for c in (7, 8, 4, 2, 1) if hidden_width % (128 * c) == 0)
+    count = next(c for c in (14, 16, 8, 4, 2) if hidden_width % (128 * c) == 0)
     chunk = hidden_width // count
-    own = total_rows // gx
+    deep = 2 * chunk
     dma = pltpu.SemaphoreType.DMA
     shape = jax.ShapeDtypeStruct
 
     buffers, sems = Reduce.scratch(gx, total_rows, chunk, count, 2)
-    fm, nm = max(far - 1, 1), max(near - 1, 1)
-    rows_all, gate_up, hidden, block_out, proj_all = pl.pallas_call(
+    fm, nm, pm = max(far - 1, 1), max(near - 1, 1), max(gx // 2 - 1, 1)
+    rows_all, hidden, gate_factor, up_factor, block_out, proj_all = pl.pallas_call(
         functools.partial(forward_kernel, gx, gy, near, count),
         in_specs=[VM, ANY, ANY, ANY, ANY],
-        out_specs=[ANY] * 5,
+        out_specs=[ANY] * 6,
         out_shape=[
             shape((total_rows, width), BF16),
-            shape((2, own, hidden_width), F32),
-            shape((1, total_rows, hidden_width), BF16),
+            shape((total_rows, hidden_width), BF16),
+            shape((total_rows, hidden_width), BF16),
+            shape((total_rows, hidden_width), BF16),
             shape((share, width), BF16),
             shape((total_rows, head_width), BF16),
         ],
         scratch_shapes=[
             pltpu.VMEM((total_rows, width), BF16),
-            pltpu.VMEM((2, own, hidden_width), F32),
+            pltpu.VMEM((2, total_rows, hidden_width), BF16),
             pltpu.VMEM((1, total_rows, hidden_width), BF16),
             pltpu.VMEM((share, width), BF16),
             pltpu.VMEM((2, total_rows, head_width // 2), BF16),
             pltpu.VMEM((2, 2, width, chunk), BF16),
-            pltpu.VMEM((2, chunk, width), BF16),
+            pltpu.VMEM((2, deep, width), BF16),
             pltpu.VMEM((width, head_width), BF16),
             pltpu.VMEM((total_rows, width), F32),
             pltpu.VMEM((2, share, head_width // 2), F32),
@@ -540,13 +586,13 @@
             dma((far, nm)), dma((far, nm)), dma((fm,)), dma((fm,)),
             dma((gx - 1,)), dma((gx - 1,)), dma((gy - 1,)), dma((gy - 1,)),
             dma((gy,)), dma((gy,)),
-            dma((2, 2)), dma((2,)), dma((1,)), dma((6,)),
+            dma((pm,)), dma((pm,)), dma((gx // 2,)), dma((gx // 2,)),
+            dma((2, 2)), dma((2,)), dma((1,)), dma((7,)),
         ],
         compiler_params=pltpu.CompilerParams(
             collective_id=0, has_side_effects=True, vmem_limit_bytes=56 << 20
         ),
     )(tokens, w_gate, w_up, w_down, w_head)
-    hidden = hidden[0]
 
     scale = 1.0 / math.sqrt(head_width)
     ids = jnp.arange(total_rows, dtype=jnp.int32)
@@ -565,30 +611,33 @@
     grad_block = contract_last(grad_proj, w_head).astype(BF16)
 
     buffers, sems = Reduce.scratch(gx, total_rows, chunk, count, 1)
-    grads, blocks = pl.pallas_call(
+    gate_grads, up_grads, blocks = pl.pallas_call(
         functools.partial(backward_kernel, gx, gy, count),
-        in_specs=[VM, VM, ANY, VM],
-        out_specs=[ANY] * 2,
+        in_specs=[VM, VM, ANY, ANY, ANY],
+        out_specs=[ANY] * 3,
         out_shape=[
-            shape((2, total_rows, hidden_width), BF16),
+            shape((total_rows, hidden_width), BF16),
+            shape((total_rows, hidden_width), BF16),
             shape((total_rows, width), BF16),
         ],
         scratch_shapes=[
-            pltpu.VMEM((2, total_rows, hidden_width), BF16),
+            pltpu.VMEM((1, total_rows, hidden_width), BF16),
             pltpu.VMEM((total_rows, width), BF16),
             pltpu.VMEM((2, chunk, width), BF16),
+            pltpu.VMEM((2, total_rows, hidden_width), BF16),
+            pltpu.VMEM((2, total_rows, hidden_width), BF16),
             *buffers,
             *sems,
-            dma((gy - 1,)), dma((gy - 1,)), dma((2,)), dma((2,)),
+            dma((gy - 1,)), dma((gy - 1,)), dma((2,)), dma((2,)), dma((3,)),
         ],
         compiler_params=pltpu.CompilerParams(
             collective_id=1, has_side_effects=True, vmem_limit_bytes=48 << 20
         ),
-    )(grad_block, block_out, w_down, gate_up)
+    )(grad_block, block_out, w_down, gate_factor, up_factor)
 
     grad_down = outer(hidden, grad_block, 256)
-    grad_gate = outer(rows_all, grads[0], 256)
-    grad_up = outer(rows_all, grads[1], 256)
+    grad_gate = outer(rows_all, gate_grads, 256)
+    grad_up = outer(rows_all, up_grads, 256)
     mine = head_width // gy
     proj_mine = lax.dynamic_slice_in_dim(grad_proj, lax.axis_index("gy") * mine, mine, 1)
     grad_head = contract_lead(blocks, proj_mine).astype(BF16)

time: 178 us -> 195 us (1.096)
  Pallas kernels: 164 us -> 183 us
  local copies, waits for them, and re-layouts: 2.97 us -> 0.68 us
    pallas_call x1, Pallas kernels: 92.1 us -> 109 us  [per_device(): pl.pallas_call(functools.partial(forward_kernel, gx, gy, near, count), in...]
    pallas_call x1, Pallas kernels: 44.5 us -> 47.3 us  [per_device(): pl.pallas_call(functools.partial(backward_kernel, gx, gy, count), in_spec...]
    squeeze x1 -> x0, local copies, waits for them, and re-layouts: 2.29 us -> none  [per_device(): grad_up = outer(rows_all, grads[1], 256)]
where the time goes in v2:
time: 195 us; the launch traced here: 194 us
  Pallas kernels  183 us (94%)
  matrix products  7.06 us (4%)
  between operations  2.52 us (1%)
    pallas_call x1, Pallas kernels, per_device(): pl.pallas_call(functools.partial(forward_kernel, gx, gy, near, count), in...  109 us
    pallas_call x1, Pallas kernels, per_device(): pl.pallas_call(functools.partial(backward_kernel, gx, gy, count), in_spec...  47.3 us
    pallas_call x3, Pallas kernels, outer(): pl.pallas_call(outer_kernel, grid=(height // tile,), in_specs=[pl.BlockSp...  27.3 us

profile of v2, /device:TPU:0, one launch (start us, length us, event | category | flops | bytes accessed | tf_op | source)
XLA Modules:
  0.0 194.4 jit_solution(13858124370581607410)
XLA Ops:
  0.6 0.0 copy-start.4
  0.6 108.9 %shard_map.109 = (bf16[256,2048]{1,0:T(8,128)(2,1)}, bf16[256,3584]{1,0:T(8,128)(2,1)}, bf16[256,3584]{1,0:T(8,128)(2,1)}, bf16[256,3584]{1,0:T(8,128)(2,1)}, bf...) custom-call(bf16[32,2048]{1,0:T(8,128)(2,1)} %tok.1, bf16[2048,3584]{1,0:T(8,128)(2,1)} %w_gate.1, ...), custom_call_target="tpu_custom_call" | custom-call | tf_op jit(solution)/shard_map/pallas_call | solution.py:554
  109.5 1.6 fusion.6
  111.1 0.0 copy-done.4
  111.1 0.1 select_reduce_fusion
  111.2 0.6 subtract_reduce_fusion
  112.5 0.0 copy-start.3
  112.5 1.5 fusion.4
  114.0 0.0 copy-start.2
  114.0 1.4 fusion.1
  115.4 0.0 copy-done.3
  115.4 1.3 convolution_convert_fusion.grad_block.right
  116.7 0.0 copy-done.2
  116.7 0.0 copy-start.1
  116.7 47.3 %shard_map.110 = (bf16[256,3584]{1,0:T(8,128)(2,1)S(1)}, bf16[256,3584]{1,0:T(8,128)(2,1)S(1)}, bf16[256,2048]{1,0:T(8,128)(2,1)S(1)}) custom-call(bf16[256,2048]{1,0:T(8,128)(2,1)S(1)} %convolution_convert_fusion.grad_block.right, bf16[32,2048]{1,0:T(8,128)(2,1)S(1)} %copy-done.2, bf16[3584,2048]{1,0:T(8,128)(2,1)} %w_down.3, ...), custom_call_target="tpu_custom_call" | custom-call | tf_op jit(solution)/shard_map/pallas_call | solution.py:614
  164.0 1.3 convolution_convert_fusion.1
  165.3 0.0 copy-done.1
  165.3 0.0 copy-start
  165.3 10.6 %shard_map.113 = bf16[3584,2048]{1,0:T(8,128)(2,1)} custom-call(bf16[256,3584]{1,0:T(8,128)(2,1)S(1)} %copy-done.1, bf16[256,2048]{1,0:T(8,128)(2,1)S(1)} %convolution_convert_fusion.grad_block.right), custom_call_target="tpu_custom_call" | custom-call | flops 3758096384 | bytes 17563648 | tf_op jit(solution)/shard_map/pallas_call | solution.py:521
  175.9 0.0 copy-done
  175.9 8.4 %shard_map.111 = bf16[2048,3584]{1,0:T(8,128)(2,1)} custom-call(bf16[256,2048]{1,0:T(8,128)(2,1)S(1)} %copy-done, bf16[256,3584]{1,0:T(8,128)(2,1)S(1)} %get-tuple-element.20.right), custom_call_target="tpu_custom_call" | custom-call | flops 3758096384 | bytes 17563648 | tf_op jit(solution)/shard_map/pallas_call | solution.py:521
  184.3 8.4 %shard_map.112 = bf16[2048,3584]{1,0:T(8,128)(2,1)} custom-call(bf16[256,2048]{1,0:T(8,128)(2,1)S(1)} %copy-done, bf16[256,3584]{1,0:T(8,128)(2,1)S(1)} %get-tuple-element.21.right), custom_call_target="tpu_custom_call" | custom-call | flops 3758096384 | bytes 17563648 | tf_op jit(solution)/shard_map/pallas_call | solution.py:521
  192.6 0.7 copy.13
Async XLA Ops:
  0.6 110.5 %copy-start.4 = (s32[256]{0:T(256)S(1)}, s32[256]{0:T(256)}, u32[]{:S(2)}) copy-start(s32[256]{0:T(256)} %param.11) | copy-start | bytes 3076
  112.5 3.0 %copy-start.3 = (bf16[2048,1024]{1,0:T(8,128)(2,1)S(1)}, bf16[2048,1024]{1,0:T(8,128)(2,1)}, u32[]{:S(2)}) copy-start(bf16[2048,1024]{1,0:T(8,128)(2,1)} %w_head.1) | copy-start | bytes 12582916
  114.0 2.7 %copy-start.2 = (bf16[32,2048]{1,0:T(8,128)(2,1)S(1)}, bf16[32,2048]{1,0:T(8,128)(2,1)}, u32[]{:S(2)}) copy-start(bf16[32,2048]{1,0:T(8,128)(2,1)} %get-tuple-element.36.block) | copy-start | bytes 393220
  116.7 48.6 %copy-start.1 = (bf16[256,3584]{1,0:T(8,128)(2,1)S(1)}, bf16[256,3584]{1,0:T(8,128)(2,1)}, u32[]{:S(2)}) copy-start(bf16[256,3584]{1,0:T(8,128)(2,1)} %get-tuple-element.22.left) | copy-start | bytes 5505028
  165.3 10.6 %copy-start = (bf16[256,2048]{1,0:T(8,128)(2,1)S(1)}, bf16[256,2048]{1,0:T(8,128)(2,1)}, u32[]{:S(2)}) copy-start(bf16[256,2048]{1,0:T(8,128)(2,1)} %get-tuple-element.17.left) | copy-start | bytes 3145732

commit v3 on v1

--- a/solution.py
+++ b/solution.py
@@ -391,7 +391,7 @@
 def backward_kernel(
     gx, gy, count,
     grad_block, block, w_down, gate_up,
-    grads_out, blocks_out,
+    gate_out, up_out, blocks_out,
     grads, blocks, w_in,
     part, snd1, rcv1, own2, snd2, rcv2,
     s1, r1, s2, r2, s3, r3, s4, r4,
@@ -454,25 +454,30 @@
         return carry
 
     lax.fori_loop(0, count, finish, 0)
-    first = pltpu.make_async_copy(grads, grads_out, store_sem.at[0])
-    first.start()
+    stores = [
+        pltpu.make_async_copy(grads.at[a], out, store_sem.at[a])
+        for a, out in enumerate((gate_out, up_out))
+    ]
+    for copy in stores:
+        copy.start()
     for o in range(1, gy):
         share_block(o, lax.rem(iy + gy - o, gy)).wait_recv()
-    second = pltpu.make_async_copy(blocks, blocks_out, store_sem.at[1])
-    second.start()
+    stores.append(pltpu.make_async_copy(blocks, blocks_out, store_sem.at[2]))
+    stores[2].start()
     for o in range(1, gy):
         share_block(o, iy).wait_send()
-    first.wait()
-    second.wait()
+    for copy in stores:
+        copy.wait()
 
 
 def outer_kernel(left, right, out):
     out[...] = contract_lead(left[...], right[...]).astype(BF16)
 
 
-def outer(left, right, tile):
+def outer(left, right):
     rows, height = left.shape
     width = right.shape[1]
+    tile = next(t for t in (512, 256, 128) if height % t == 0)
     return pl.pallas_call(
         outer_kernel,
         grid=(height // tile,),
@@ -565,12 +570,13 @@
     grad_block = contract_last(grad_proj, w_head).astype(BF16)
 
     buffers, sems = Reduce.scratch(gx, total_rows, chunk, count, 1)
-    grads, blocks = pl.pallas_call(
+    gate_grads, up_grads, blocks = pl.pallas_call(
         functools.partial(backward_kernel, gx, gy, count),
         in_specs=[VM, VM, ANY, VM],
-        out_specs=[ANY] * 2,
+        out_specs=[ANY] * 3,
         out_shape=[
-            shape((2, total_rows, hidden_width), BF16),
+            shape((total_rows, hidden_width), BF16),
+            shape((total_rows, hidden_width), BF16),
             shape((total_rows, width), BF16),
         ],
         scratch_shapes=[
@@ -579,16 +585,16 @@
             pltpu.VMEM((2, chunk, width), BF16),
             *buffers,
             *sems,
-            dma((gy - 1,)), dma((gy - 1,)), dma((2,)), dma((2,)),
+            dma((gy - 1,)), dma((gy - 1,)), dma((2,)), dma((3,)),
         ],
         compiler_params=pltpu.CompilerParams(
             collective_id=1, has_side_effects=True, vmem_limit_bytes=48 << 20
         ),
     )(grad_block, block_out, w_down, gate_up)
 
-    grad_down = outer(hidden, grad_block, 256)
-    grad_gate = outer(rows_all, grads[0], 256)
-    grad_up = outer(rows_all, grads[1], 256)
+    grad_down = outer(hidden, grad_block)
+    grad_gate = outer(rows_all, gate_grads)
+    grad_up = outer(rows_all, up_grads)
     mine = head_width // gy
     proj_mine = lax.dynamic_slice_in_dim(grad_proj, lax.axis_index("gy") * mine, mine, 1)
     grad_head = contract_lead(blocks, proj_mine).astype(BF16)

time: 178 us -> 171 us (0.961)
  Pallas kernels: 164 us -> 160 us
  local copies, waits for them, and re-layouts: 2.97 us -> 0.68 us
    pallas_call x3, Pallas kernels: 27.3 us -> 22.7 us  [outer(): pl.pallas_call(outer_kernel, grid=(height // tile,), in_specs=[pl.BlockSp...]
    squeeze x1 -> x0, local copies, waits for them, and re-layouts: 2.29 us -> none  [per_device(): grad_up = outer(rows_all, grads[1], 256)]
where the time goes in v3:
time: 171 us; the launch traced here: 170 us
  Pallas kernels  160 us (94%)
  matrix products  7.07 us (4%)
  between operations  2.52 us (1%)
    pallas_call x1, Pallas kernels, per_device(): pl.pallas_call(functools.partial(forward_kernel, gx, gy, near, count), in...  92.1 us
    pallas_call x1, Pallas kernels, per_device(): pl.pallas_call(functools.partial(backward_kernel, gx, gy, count), in_spec...  44.6 us
    pallas_call x3, Pallas kernels, outer(): pl.pallas_call(outer_kernel, grid=(height // tile,), in_specs=[pl.BlockSp...  22.7 us

profile of v3, /device:TPU:0, one launch (start us, length us, event | category | flops | bytes accessed | tf_op | source)
XLA Modules:
  0.0 170.5 jit_solution(11303470670134900928)
XLA Ops:
  0.6 0.0 copy-start.4
  0.6 92.1 %shard_map.109 = (bf16[256,2048]{1,0:T(8,128)(2,1)}, f32[2,64,3584]{2,1,0:T(8,128)}, bf16[1,256,3584]{2,1,0:T(8,128)(2,1)}, bf16[32,2048]{1,0:T(8,128)(2,1)}, bf16[256,1024]{1,0:T(8,128)(2,1)}) custom-call(bf16[32,2048]{1,0:T(8,128)(2,1)} %tok.1, bf16[2048,3584]{1,0:T(8,128)(2,1)} %w_gate.1, bf16[2048,3584]{1,0:T(8,128)(2,1)} %w_up.1, ...), custom_call_target="tpu_custom_call" | custom-call | tf_op jit(solution)/shard_map/pallas_call | solution.py:514
  92.8 1.6 fusion.6
  94.3 0.0 copy-done.4
  94.3 0.1 select_reduce_fusion
  94.4 0.6 subtract_reduce_fusion
  95.7 0.0 copy-start.3
  95.7 1.5 fusion.4
  97.3 0.0 copy-start.2
  97.3 1.4 fusion.1
  98.7 0.0 copy-done.3
  98.7 1.3 convolution_convert_fusion.grad_block.right
  100.0 0.0 copy-done.2
  100.0 0.0 copy-start.1
  100.0 44.6 %shard_map.110 = (bf16[256,3584]{1,0:T(8,128)(2,1)S(1)}, bf16[256,3584]{1,0:T(8,128)(2,1)S(1)}, bf16[256,2048]{1,0:T(8,128)(2,1)S(1)}) custom-call(bf16[256,2048]{1,0:T(8,128)(2,1)S(1)} %convolution_convert_fusion.grad_block.right, bf16[32,2048]{1,0:T(8,128)(2,1)S(1)} %copy-done.2, bf16[3584,2048]{1,0:T(8,128)(2,1)} %w_down.3, ...), custom_call_target="tpu_custom_call" | custom-call | tf_op jit(solution)/shard_map/pallas_call | solution.py:573
  144.6 1.3 convolution_convert_fusion.1
  145.9 0.0 copy-done.1
  145.9 0.0 copy-start
  145.9 8.3 %shard_map.113 = bf16[3584,2048]{1,0:T(8,128)(2,1)} custom-call(bf16[256,3584]{1,0:T(8,128)(2,1)S(1)} %bitcast.8, bf16[256,2048]{1,0:T(8,128)(2,1)S(1)} %convolution_convert_fusion.grad_block.right), custom_call_target="tpu_custom_call" | custom-call | flops 3758096384 | bytes 17563648 | tf_op jit(solution)/shard_map/pallas_call | solution.py:481
  154.2 0.0 copy-done
  154.2 7.2 %shard_map.111 = bf16[2048,3584]{1,0:T(8,128)(2,1)} custom-call(bf16[256,2048]{1,0:T(8,128)(2,1)S(1)} %copy-done, bf16[256,3584]{1,0:T(8,128)(2,1)S(1)} %get-tuple-element.18.right), custom_call_target="tpu_custom_call" | custom-call | flops 3758096384 | bytes 17563648 | tf_op jit(solution)/shard_map/pallas_call | solution.py:481
  161.5 7.2 %shard_map.112 = bf16[2048,3584]{1,0:T(8,128)(2,1)} custom-call(bf16[256,2048]{1,0:T(8,128)(2,1)S(1)} %copy-done, bf16[256,3584]{1,0:T(8,128)(2,1)S(1)} %get-tuple-element.19.right), custom_call_target="tpu_custom_call" | custom-call | flops 3758096384 | bytes 17563648 | tf_op jit(solution)/shard_map/pallas_call | solution.py:481
  168.7 0.7 copy.13
Async XLA Ops:
  0.6 93.7 %copy-start.4 = (s32[256]{0:T(256)S(1)}, s32[256]{0:T(256)}, u32[]{:S(2)}) copy-start(s32[256]{0:T(256)} %param.11) | copy-start | bytes 3076
  95.7 3.0 %copy-start.3 = (bf16[2048,1024]{1,0:T(8,128)(2,1)S(1)}, bf16[2048,1024]{1,0:T(8,128)(2,1)}, u32[]{:S(2)}) copy-start(bf16[2048,1024]{1,0:T(8,128)(2,1)} %w_head.1) | copy-start | bytes 12582916
  97.3 2.7 %copy-start.2 = (bf16[32,2048]{1,0:T(8,128)(2,1)S(1)}, bf16[32,2048]{1,0:T(8,128)(2,1)}, u32[]{:S(2)}) copy-start(bf16[32,2048]{1,0:T(8,128)(2,1)} %get-tuple-element.34.block) | copy-start | bytes 393220
  100.0 46.0 %copy-start.1 = (bf16[1,256,3584]{2,1,0:T(8,128)(2,1)S(1)}, bf16[1,256,3584]{2,1,0:T(8,128)(2,1)}, u32[]{:S(2)}) copy-start(bf16[1,256,3584]{2,1,0:T(8,128)(2,1)} %get-tuple-element.20) | copy-start | bytes 5505028
  145.9 8.3 %copy-start = (bf16[256,2048]{1,0:T(8,128)(2,1)S(1)}, bf16[256,2048]{1,0:T(8,128)(2,1)}, u32[]{:S(2)}) copy-start(bf16[256,2048]{1,0:T(8,128)(2,1)} %get-tuple-element.16.left) | copy-start | bytes 3145732
